TPU v7x, 32 devices: a whole 2x2x4 slice. The times are simulated.
32 devices in a mesh: parts: 2 (over y), leaf: 4 (over z), sub: 4 (over x, core).
Axes of the slice: x: 2, y: 2, z: 4, core: 2. Of those that a mesh axis runs over, the one named last changes fastest.
Arguments:
- points: float32 [6, 65536], P(None, ('parts', 'leaf', 'sub')), parts along dimension 1
- targets: float32 [64, 65536], P(None, ('parts', 'leaf', 'sub')), parts along dimension 1
- leaf_skel: int32 [32, 256], P(('parts', 'leaf', 'sub')), parts along dimension 0, may hold values from 0 to 2047, as said below
- node_keep: int32 [30, 256], P('parts'), parts along dimension 0, may hold values from 0 to 511, as said below
- lengthscales: float32 [12], P('parts'), parts along dimension 0, may hold values from 0.25 to 0.35
- noise_var: float32 [2], P('parts'), parts along dimension 0, may hold values from 0.5 to 1.5
Outputs:
- solution: float32 [64, 65536], P(None, ('parts', 'leaf', 'sub')), parts along dimension 1
- residual: float32 [64, 65536], P(None, ('parts', 'leaf', 'sub')), parts along dimension 1
There are 2 independent parts, one for each index of `parts`. A program takes and returns all parts, laid end to end along the dimension named above; each array names one. Nothing has to cross between parts.
Inputs may be any that keep to these rules, and one draw needn't show every extreme that they name: `leaf_skel`: row t lists 256 distinct positions among the 2048 points of leaf t. `node_keep`: row n lists 256 distinct positions in the concatenation of the skeletons of heap nodes 2n+1 and 2n+2, the first node's 256 points before the second's.
All inputs are finite; a program needn't handle non-finite values.
Results may differ from a plain program's by a relative error of at most 0.0004.
Values sent between devices are 32-bit elements; how exact they have to be, the bound alone decides.
No kernel may reach another device: no remote copies, remote signals or barrier semaphores. Data moves between devices by JAX's collectives and lax.ppermute only.
A program may use at most 128 MiB of HBM per device.

v0:
```python
import jax
import jax.numpy as jnp
from jax import lax
from jax.sharding import PartitionSpec as P

ITERS = 3


def from_partner(shard, axis, stride):
    return lax.ppermute(shard, axis, [(i, i ^ 1 << stride) for i in range(lax.axis_size(axis))])


def kernel(left, right, inverse_scale):
    squared = jnp.zeros((left.shape[1], right.shape[1]), jnp.float32)
    for axis_number in range(left.shape[0]):
        offset = (left[axis_number][:, None] - right[axis_number][None, :]) * inverse_scale[
            axis_number
        ]
        squared = squared + offset * offset
    return jnp.exp(-0.5 * squared)


def product(first, second):
    return jnp.dot(
        first, second, precision=lax.Precision.HIGHEST, preferred_element_type=jnp.float32
    )


def merged(own_part, their_part, on_right):
    return jnp.concatenate(
        [jnp.where(on_right, their_part, own_part), jnp.where(on_right, own_part, their_part)],
        axis=-1,
    )


def climb_up(packed, sibling, on_right, chosen, dims, inverse_scale):
    joined = merged(packed, sibling, on_right)
    joined_coords = joined[:dims]
    parent = jnp.take(joined_coords, chosen, axis=1)
    transfer = kernel(joined_coords, parent, inverse_scale)
    return (parent, product(joined[dims:], transfer), transfer)


def body(points, targets, leaf_skel, node_keep, lengthscales, noise_var):
    dims = points.shape[0]
    leaf_size = points.shape[1]
    skeleton_rank = leaf_skel.shape[1]
    rhs_count = targets.shape[0]
    inverse_scale = 1.0 / lengthscales
    sub_count = lax.axis_size("sub")
    leaf_count = lax.axis_size("leaf")
    sub_levels = sub_count.bit_length() - 1
    levels = sub_levels + leaf_count.bit_length() - 1
    leaf_number = lax.axis_index("leaf") * sub_count + lax.axis_index("sub")
    own_coords = jnp.take(points, leaf_skel[0], axis=1)
    leaf_basis = kernel(points, own_coords, inverse_scale)
    block_width = min(256, leaf_size)
    blocks = leaf_size // block_width

    def pick_rows(tree_level):
        heap_index = (1 << levels - tree_level) - 1 + (leaf_number >> tree_level)
        return lax.dynamic_index_in_dim(node_keep, heap_index, 0, keepdims=False)

    def side_of(tree_level):
        return leaf_number >> tree_level - 1 & 1 == 1

    solution = jnp.zeros_like(targets)
    residual = targets
    direction = targets
    norm_now = lax.psum(jnp.sum(residual * residual, axis=1), ("leaf", "sub"))
    for iteration in range(ITERS):
        node_weight = product(direction, leaf_basis)
        coords = own_coords
        ancestry = []
        for apply_tree_level in range(1, sub_levels + 1):
            on_right = side_of(apply_tree_level)
            packed = jnp.concatenate([coords, node_weight], axis=0)
            sibling = from_partner(packed, "sub", apply_tree_level - 1)
            crossing = kernel(sibling[:dims], coords, inverse_scale)
            sibling_w = sibling[dims:]
            coords, node_weight, transfer = climb_up(
                packed, sibling, on_right, pick_rows(apply_tree_level), dims, inverse_scale
            )
            ancestry.append((transfer, crossing, sibling_w, on_right))
        for apply_tree_level in range(sub_levels + 1, levels + 1):
            on_right = side_of(apply_tree_level)
            packed = jnp.concatenate([coords, node_weight], axis=0)
            sibling = from_partner(packed, "leaf", apply_tree_level - 1 - sub_levels)
            crossing = kernel(sibling[:dims], coords, inverse_scale)
            sibling_w = sibling[dims:]
            coords, node_weight, transfer = climb_up(
                packed, sibling, on_right, pick_rows(apply_tree_level), dims, inverse_scale
            )
            ancestry.append((transfer, crossing, sibling_w, on_right))
        search_vector = jnp.zeros((rhs_count, skeleton_rank), jnp.float32)
        for apply_tree_level in range(levels, 0, -1):
            transfer, crossing, sibling_w, on_right = ancestry[apply_tree_level - 1]
            downward_sweep = product(search_vector, transfer.T)
            own_half = jnp.where(
                on_right, downward_sweep[:, skeleton_rank:], downward_sweep[:, :skeleton_rank]
            )
            search_vector = product(sibling_w, crossing) + own_half
        far_term = product(search_vector, leaf_basis.T)
        values = direction

        def one_block(block_index):
            columns = lax.dynamic_slice_in_dim(points, block_index * block_width, block_width, 1)
            return product(values, kernel(points, columns, inverse_scale))

        pieces = lax.map(one_block, jnp.arange(blocks))
        image = noise_var[0] * direction + (
            jnp.transpose(pieces, (1, 0, 2)).reshape(values.shape[0], leaf_size) + far_term
        )
        curve = lax.psum(jnp.sum(direction * image, axis=1), ("leaf", "sub"))
        step_size = norm_now / curve
        solution = solution + step_size[:, None] * direction
        residual = residual - step_size[:, None] * image
        if iteration + 1 < ITERS:
            norm_next = lax.psum(jnp.sum(residual * residual, axis=1), ("leaf", "sub"))
        if iteration + 1 < ITERS:
            direction = residual + (norm_next / norm_now)[:, None] * direction
            norm_now = norm_next
    return (solution, residual)


def solution(mesh):
    in_specs = (
        P(None, ("parts", "leaf", "sub")),
        P(None, ("parts", "leaf", "sub")),
        P(("parts", "leaf", "sub"), None),
        P("parts", None),
        P("parts"),
        P("parts"),
    )
    out_specs = (P(None, ("parts", "leaf", "sub")), P(None, ("parts", "leaf", "sub")))
    return jax.shard_map(body, mesh=mesh, in_specs=in_specs, out_specs=out_specs, check_vma=False)
```

profile of v0, /device:TPU:0, one launch (start us, length us, event | category | flops | bytes accessed | tf_op | source)
XLA Modules:
  0.0 633.5 jit_solution(1695092716191772870)
XLA Ops:
  4.5 7.0 %convolution_bitcast_fusion = f32[64,256]{1,0:T(8,128)S(1)} fusion(f32[64,2048]{1,0:T(8,128)S(1)} %copy-done.1, f32[]{:T(128)} %bitcast.86, f32[256]{0:T(256)S(1)} %bitcast.707, f32[2048]{0:T(1024)S(1)} %bitcast.534, f32[]{:T(128)} %bitcast.83, f32[256]{0:T(256)S(1)} %bitcast.716, f32[2048]{0:T(1024)S(1)} %bitcast.540, f32[]{:T(128)} %bitcast.80, ...), kind=kOutput, calls=%fused_computation.179 | convolution fusion | flops 415236096 | bytes 645144 | tf_op jit(solution)/shard_map/dot_general | solution.py:24
  12.3 72.7 %while.30 = (s32[]{:T(128)}, f32[8,64,256]{2,1,0:T(8,128)S(1)}, f32[6,2048]{1,0:T(8,128)S(1)}, s32[8]{0:T(128)S(1)}, f32[6]{0:T(128)S(1)}, /*index=5*/f32[64,204...) while((s32[]{:T(128)}, f32[8,64,256]{2,1,0:T(8,128)S(1)}, ...), condition=%wide.region_3.4_spmd, body=%wide.region_2.3_spmd.sunk | while | flops 415236096 | bytes 756071 | solution.py:110
  14.4 6.9 %fusion.1032 = f32[8,64,256]{2,1,0:T(8,128)S(1)} fusion(f32[8,64,256]{2,1,0:T(8,128)S(1)} %get-tuple-element.708, s32[]{:T(128)} %get-tuple-element.707, f32[64,2048]{1,0:T(8,128)S(1)} %get-tuple-element.727, f32[]{:T(128)} %bitcast.420, f32[256]{0:T(256)S(1)} %bitcast.513, f32[2048]{0:T(1024)S(1)} %bitcast.491, f32[]{:T(128)} %bitcast.424, ...), kind=kOutput, calls=%fused_computation.40.clone.1 | convolution fusion | flops 415236096 | bytes 645148 | tf_op jit(solution)/shard_map/while/body/eval_jaxpr/dot_general | solution.py:24
  23.5 6.9 %fusion.1032 = f32[8,64,256]{2,1,0:T(8,128)S(1)} fusion(f32[8,64,256]{2,1,0:T(8,128)S(1)} %get-tuple-element.708, s32[]{:T(128)} %get-tuple-element.707, f32[64,2048]{1,0:T(8,128)S(1)} %get-tuple-element.727, f32[]{:T(128)} %bitcast.420, f32[256]{0:T(256)S(1)} %bitcast.513, f32[2048]{0:T(1024)S(1)} %bitcast.491, f32[]{:T(128)} %bitcast.424, ...), kind=kOutput, calls=%fused_computation.40.clone.1 | convolution fusion | flops 415236096 | bytes 645148 | tf_op jit(solution)/shard_map/while/body/eval_jaxpr/dot_general | solution.py:24
  32.5 6.9 %fusion.1032 = f32[8,64,256]{2,1,0:T(8,128)S(1)} fusion(f32[8,64,256]{2,1,0:T(8,128)S(1)} %get-tuple-element.708, s32[]{:T(128)} %get-tuple-element.707, f32[64,2048]{1,0:T(8,128)S(1)} %get-tuple-element.727, f32[]{:T(128)} %bitcast.420, f32[256]{0:T(256)S(1)} %bitcast.513, f32[2048]{0:T(1024)S(1)} %bitcast.491, f32[]{:T(128)} %bitcast.424, ...), kind=kOutput, calls=%fused_computation.40.clone.1 | convolution fusion | flops 415236096 | bytes 645148 | tf_op jit(solution)/shard_map/while/body/eval_jaxpr/dot_general | solution.py:24
  41.6 6.9 %fusion.1032 = f32[8,64,256]{2,1,0:T(8,128)S(1)} fusion(f32[8,64,256]{2,1,0:T(8,128)S(1)} %get-tuple-element.708, s32[]{:T(128)} %get-tuple-element.707, f32[64,2048]{1,0:T(8,128)S(1)} %get-tuple-element.727, f32[]{:T(128)} %bitcast.420, f32[256]{0:T(256)S(1)} %bitcast.513, f32[2048]{0:T(1024)S(1)} %bitcast.491, f32[]{:T(128)} %bitcast.424, ...), kind=kOutput, calls=%fused_computation.40.clone.1 | convolution fusion | flops 415236096 | bytes 645148 | tf_op jit(solution)/shard_map/while/body/eval_jaxpr/dot_general | solution.py:24
  50.7 6.9 %fusion.1032 = f32[8,64,256]{2,1,0:T(8,128)S(1)} fusion(f32[8,64,256]{2,1,0:T(8,128)S(1)} %get-tuple-element.708, s32[]{:T(128)} %get-tuple-element.707, f32[64,2048]{1,0:T(8,128)S(1)} %get-tuple-element.727, f32[]{:T(128)} %bitcast.420, f32[256]{0:T(256)S(1)} %bitcast.513, f32[2048]{0:T(1024)S(1)} %bitcast.491, f32[]{:T(128)} %bitcast.424, ...), kind=kOutput, calls=%fused_computation.40.clone.1 | convolution fusion | flops 415236096 | bytes 645148 | tf_op jit(solution)/shard_map/while/body/eval_jaxpr/dot_general | solution.py:24
  59.7 6.9 %fusion.1032 = f32[8,64,256]{2,1,0:T(8,128)S(1)} fusion(f32[8,64,256]{2,1,0:T(8,128)S(1)} %get-tuple-element.708, s32[]{:T(128)} %get-tuple-element.707, f32[64,2048]{1,0:T(8,128)S(1)} %get-tuple-element.727, f32[]{:T(128)} %bitcast.420, f32[256]{0:T(256)S(1)} %bitcast.513, f32[2048]{0:T(1024)S(1)} %bitcast.491, f32[]{:T(128)} %bitcast.424, ...), kind=kOutput, calls=%fused_computation.40.clone.1 | convolution fusion | flops 415236096 | bytes 645148 | tf_op jit(solution)/shard_map/while/body/eval_jaxpr/dot_general | solution.py:24
  68.8 6.9 %fusion.1032 = f32[8,64,256]{2,1,0:T(8,128)S(1)} fusion(f32[8,64,256]{2,1,0:T(8,128)S(1)} %get-tuple-element.708, s32[]{:T(128)} %get-tuple-element.707, f32[64,2048]{1,0:T(8,128)S(1)} %get-tuple-element.727, f32[]{:T(128)} %bitcast.420, f32[256]{0:T(256)S(1)} %bitcast.513, f32[2048]{0:T(1024)S(1)} %bitcast.491, f32[]{:T(128)} %bitcast.424, ...), kind=kOutput, calls=%fused_computation.40.clone.1 | convolution fusion | flops 415236096 | bytes 645148 | tf_op jit(solution)/shard_map/while/body/eval_jaxpr/dot_general | solution.py:24
  77.9 6.9 %fusion.1032 = f32[8,64,256]{2,1,0:T(8,128)S(1)} fusion(f32[8,64,256]{2,1,0:T(8,128)S(1)} %get-tuple-element.708, s32[]{:T(128)} %get-tuple-element.707, f32[64,2048]{1,0:T(8,128)S(1)} %get-tuple-element.727, f32[]{:T(128)} %bitcast.420, f32[256]{0:T(256)S(1)} %bitcast.513, f32[2048]{0:T(1024)S(1)} %bitcast.491, f32[]{:T(128)} %bitcast.424, ...), kind=kOutput, calls=%fused_computation.40.clone.1 | convolution fusion | flops 415236096 | bytes 645148 | tf_op jit(solution)/shard_map/while/body/eval_jaxpr/dot_general | solution.py:24
  119.7 4.9 fusion.211
  138.1 4.9 fusion.569
  156.5 8.1 %multiply_reduce_fusion.4 = (f32[64]{0:T(128)S(1)}, f32[64]{0:T(128)S(1)}, f32[64,2048]{1,0:T(8,128)S(1)}) fusion(f32[64,2048]{1,0:T(8,128)S(1)} %get-tuple-element.829, f32[64,2048]{1,0:T(8,128)S(1)} %bitcast.488, f32[64,256]{1,0:T(8,128)S(1)} %convolution_add_fusion.14, f32[]{:T(128)} %bitcast.86, f32[256]{0:T(256)S(1)} %bitcast.709, ...), kind=kOutput, calls=%fused_computation.248 | convolution fusion | flops 416153472 | bytes 1694236 | tf_op jit(solution)/shard_map/dot_general | solution.py:24
  164.5 31.9 %all-reduce = (f32[64]{0:T(128)S(1)}, f32[64]{0:T(128)S(1)}) all-reduce(f32[64]{0:T(128)S(1)} %get-tuple-element.103, f32[64]{0:T(128)S(1)} %get-tuple-element.102), channel_id=1, replica_groups=mesh['parts'=2,'leaf'=4,'sub'=4] {'leaf','sub'}, use_global_device_ids=true, to_apply=%region_1.2 | all-reduce | flops 128 | bytes 1024 | tf_op jit(solution)/shard_map/psum | solution.py:70
  196.7 29.5 %psum.44 = f32[64]{0:T(128)S(1)} all-reduce(f32[64]{0:T(128)S(1)} %multiply_reduce_fusion.3), channel_id=1, replica_groups=mesh['parts'=2,'leaf'=4,'sub'=4] {'leaf','sub'}, use_global_device_ids=true, to_apply=%region_7.9 | all-reduce | flops 64 | bytes 512 | tf_op jit(solution)/shard_map/psum | solution.py:119
  226.4 6.8 %fusion.964 = f32[64,256]{1,0:T(8,128)S(1)} fusion(f32[64,2048]{1,0:T(8,128)S(1)} %multiply_add_fusion.2, f32[]{:T(128)} %bitcast.86, f32[256]{0:T(256)S(1)} %bitcast.710, f32[2048]{0:T(1024)S(1)} %bitcast.536, f32[]{:T(128)} %bitcast.83, f32[256]{0:T(256)S(1)} %bitcast.719, f32[2048]{0:T(1024)S(1)} %bitcast.542, f32[]{:T(128)} %bitcast.80, ...), kind=kOutput, calls=%fused_computation.1244 | convolution fusion | flops 415236096 | bytes 645144 | tf_op jit(solution)/shard_map/dot_general | solution.py:24
  233.3 72.7 %while.31 = (s32[]{:T(128)}, f32[8,64,256]{2,1,0:T(8,128)S(1)}, f32[6,2048]{1,0:T(8,128)S(1)}, s32[8]{0:T(128)S(1)}, f32[6]{0:T(128)S(1)}, /*index=5*/f32[64,204...) while((s32[]{:T(128)}, f32[8,64,256]{2,1,0:T(8,128)S(1)}, ...), condition=%wide.region_9.11_spmd, body=%wide.region_8.10_spmd.sunk | while | flops 415236096 | bytes 756071 | solution.py:110
  235.5 6.9 %fusion.1037 = f32[8,64,256]{2,1,0:T(8,128)S(1)} fusion(f32[8,64,256]{2,1,0:T(8,128)S(1)} %get-tuple-element.753, s32[]{:T(128)} %get-tuple-element.752, f32[64,2048]{1,0:T(8,128)S(1)} %get-tuple-element.772, f32[]{:T(128)} %bitcast.441, f32[256]{0:T(256)S(1)} %bitcast.519, f32[2048]{0:T(1024)S(1)} %bitcast.497, f32[]{:T(128)} %bitcast.445, ...), kind=kOutput, calls=%fused_computation.89.clone.1 | convolution fusion | flops 415236096 | bytes 645148 | tf_op jit(solution)/shard_map/while/body/eval_jaxpr/dot_general | solution.py:24
  244.6 6.9 %fusion.1037 = f32[8,64,256]{2,1,0:T(8,128)S(1)} fusion(f32[8,64,256]{2,1,0:T(8,128)S(1)} %get-tuple-element.753, s32[]{:T(128)} %get-tuple-element.752, f32[64,2048]{1,0:T(8,128)S(1)} %get-tuple-element.772, f32[]{:T(128)} %bitcast.441, f32[256]{0:T(256)S(1)} %bitcast.519, f32[2048]{0:T(1024)S(1)} %bitcast.497, f32[]{:T(128)} %bitcast.445, ...), kind=kOutput, calls=%fused_computation.89.clone.1 | convolution fusion | flops 415236096 | bytes 645148 | tf_op jit(solution)/shard_map/while/body/eval_jaxpr/dot_general | solution.py:24
  253.6 6.9 %fusion.1037 = f32[8,64,256]{2,1,0:T(8,128)S(1)} fusion(f32[8,64,256]{2,1,0:T(8,128)S(1)} %get-tuple-element.753, s32[]{:T(128)} %get-tuple-element.752, f32[64,2048]{1,0:T(8,128)S(1)} %get-tuple-element.772, f32[]{:T(128)} %bitcast.441, f32[256]{0:T(256)S(1)} %bitcast.519, f32[2048]{0:T(1024)S(1)} %bitcast.497, f32[]{:T(128)} %bitcast.445, ...), kind=kOutput, calls=%fused_computation.89.clone.1 | convolution fusion | flops 415236096 | bytes 645148 | tf_op jit(solution)/shard_map/while/body/eval_jaxpr/dot_general | solution.py:24
  262.7 6.9 %fusion.1037 = f32[8,64,256]{2,1,0:T(8,128)S(1)} fusion(f32[8,64,256]{2,1,0:T(8,128)S(1)} %get-tuple-element.753, s32[]{:T(128)} %get-tuple-element.752, f32[64,2048]{1,0:T(8,128)S(1)} %get-tuple-element.772, f32[]{:T(128)} %bitcast.441, f32[256]{0:T(256)S(1)} %bitcast.519, f32[2048]{0:T(1024)S(1)} %bitcast.497, f32[]{:T(128)} %bitcast.445, ...), kind=kOutput, calls=%fused_computation.89.clone.1 | convolution fusion | flops 415236096 | bytes 645148 | tf_op jit(solution)/shard_map/while/body/eval_jaxpr/dot_general | solution.py:24
  271.7 6.9 %fusion.1037 = f32[8,64,256]{2,1,0:T(8,128)S(1)} fusion(f32[8,64,256]{2,1,0:T(8,128)S(1)} %get-tuple-element.753, s32[]{:T(128)} %get-tuple-element.752, f32[64,2048]{1,0:T(8,128)S(1)} %get-tuple-element.772, f32[]{:T(128)} %bitcast.441, f32[256]{0:T(256)S(1)} %bitcast.519, f32[2048]{0:T(1024)S(1)} %bitcast.497, f32[]{:T(128)} %bitcast.445, ...), kind=kOutput, calls=%fused_computation.89.clone.1 | convolution fusion | flops 415236096 | bytes 645148 | tf_op jit(solution)/shard_map/while/body/eval_jaxpr/dot_general | solution.py:24
  280.8 6.9 %fusion.1037 = f32[8,64,256]{2,1,0:T(8,128)S(1)} fusion(f32[8,64,256]{2,1,0:T(8,128)S(1)} %get-tuple-element.753, s32[]{:T(128)} %get-tuple-element.752, f32[64,2048]{1,0:T(8,128)S(1)} %get-tuple-element.772, f32[]{:T(128)} %bitcast.441, f32[256]{0:T(256)S(1)} %bitcast.519, f32[2048]{0:T(1024)S(1)} %bitcast.497, f32[]{:T(128)} %bitcast.445, ...), kind=kOutput, calls=%fused_computation.89.clone.1 | convolution fusion | flops 415236096 | bytes 645148 | tf_op jit(solution)/shard_map/while/body/eval_jaxpr/dot_general | solution.py:24
  289.9 6.9 %fusion.1037 = f32[8,64,256]{2,1,0:T(8,128)S(1)} fusion(f32[8,64,256]{2,1,0:T(8,128)S(1)} %get-tuple-element.753, s32[]{:T(128)} %get-tuple-element.752, f32[64,2048]{1,0:T(8,128)S(1)} %get-tuple-element.772, f32[]{:T(128)} %bitcast.441, f32[256]{0:T(256)S(1)} %bitcast.519, f32[2048]{0:T(1024)S(1)} %bitcast.497, f32[]{:T(128)} %bitcast.445, ...), kind=kOutput, calls=%fused_computation.89.clone.1 | convolution fusion | flops 415236096 | bytes 645148 | tf_op jit(solution)/shard_map/while/body/eval_jaxpr/dot_general | solution.py:24
  298.9 6.9 %fusion.1037 = f32[8,64,256]{2,1,0:T(8,128)S(1)} fusion(f32[8,64,256]{2,1,0:T(8,128)S(1)} %get-tuple-element.753, s32[]{:T(128)} %get-tuple-element.752, f32[64,2048]{1,0:T(8,128)S(1)} %get-tuple-element.772, f32[]{:T(128)} %bitcast.441, f32[256]{0:T(256)S(1)} %bitcast.519, f32[2048]{0:T(1024)S(1)} %bitcast.497, f32[]{:T(128)} %bitcast.445, ...), kind=kOutput, calls=%fused_computation.89.clone.1 | convolution fusion | flops 415236096 | bytes 645148 | tf_op jit(solution)/shard_map/while/body/eval_jaxpr/dot_general | solution.py:24
  332.6 5.5 collective-permute-done.7
  339.6 4.9 fusion.185
  348.8 4.9 fusion.577
  358.0 4.9 fusion.575
  367.2 4.9 fusion.573
  376.3 7.9 %multiply_reduce_fusion.2 = (f32[64]{0:T(128)S(1)}, f32[64,2048]{1,0:T(8,128)S(1)}) fusion(f32[64,2048]{1,0:T(8,128)S(1)} %get-tuple-element.832, f32[64,2048]{1,0:T(8,128)S(1)} %bitcast.489, f32[64,256]{1,0:T(8,128)S(1)} %convolution_add_fusion.10, f32[]{:T(128)} %bitcast.86, f32[256]{0:T(256)S(1)} %bitcast.712, f32[2048]{0:T(1024)S(1)} %bitcast.537, ...), kind=kOutput, calls=%fused_computation.215 | convolution fusion | flops 415891392 | bytes 1693980 | tf_op jit(solution)/shard_map/dot_general | solution.py:24
  384.2 29.5 %psum.45 = f32[64]{0:T(128)S(1)} all-reduce(f32[64]{0:T(128)S(1)} %get-tuple-element.463), channel_id=1, replica_groups=mesh['parts'=2,'leaf'=4,'sub'=4] {'leaf','sub'}, use_global_device_ids=true, to_apply=%region_11.13 | all-reduce | flops 64 | bytes 512 | tf_op jit(solution)/shard_map/psum | solution.py:114
  414.3 29.5 %psum.46 = f32[64]{0:T(128)S(1)} all-reduce(f32[64]{0:T(128)S(1)} %get-tuple-element.160), channel_id=1, replica_groups=mesh['parts'=2,'leaf'=4,'sub'=4] {'leaf','sub'}, use_global_device_ids=true, to_apply=%region_13.15 | all-reduce | flops 64 | bytes 512 | tf_op jit(solution)/shard_map/psum | solution.py:119
  444.5 6.8 %fusion.963 = f32[64,256]{1,0:T(8,128)S(1)} fusion(f32[64,2048]{1,0:T(8,128)S(1)} %multiply_add_fusion.1, f32[]{:T(128)} %bitcast.86, f32[256]{0:T(256)S(1)} %bitcast.713, f32[2048]{0:T(1024)S(1)} %bitcast.538, f32[]{:T(128)} %bitcast.83, f32[256]{0:T(256)S(1)} %bitcast.722, f32[2048]{0:T(1024)S(1)} %bitcast.544, f32[]{:T(128)} %bitcast.80, ...), kind=kOutput, calls=%fused_computation.1243 | convolution fusion | flops 415236096 | bytes 645144 | tf_op jit(solution)/shard_map/dot_general | solution.py:24
  451.4 72.2 %while.32 = (s32[]{:T(128)}, f32[8,64,256]{2,1,0:T(8,128)S(1)}, f32[6,2048]{1,0:T(8,128)S(1)}, s32[8]{0:T(128)S(1)}, f32[6]{0:T(128)S(1)}, /*index=5*/f32[64,204...) while((s32[]{:T(128)}, f32[8,64,256]{2,1,0:T(8,128)S(1)}, ...), condition=%wide.region_15.17_spmd, body=%wide.region_14.16_spmd.sunk | while | flops 415236096 | bytes 756071 | solution.py:110
  453.5 6.9 %fusion.1042 = f32[8,64,256]{2,1,0:T(8,128)S(1)} fusion(f32[8,64,256]{2,1,0:T(8,128)S(1)} %get-tuple-element.798, s32[]{:T(128)} %get-tuple-element.797, f32[64,2048]{1,0:T(8,128)S(1)} %get-tuple-element.817, f32[]{:T(128)} %bitcast.462, f32[256]{0:T(256)S(1)} %bitcast.525, f32[2048]{0:T(1024)S(1)} %bitcast.503, f32[]{:T(128)} %bitcast.466, ...), kind=kOutput, calls=%fused_computation.138.clone.1 | convolution fusion | flops 415236096 | bytes 645148 | tf_op jit(solution)/shard_map/while/body/eval_jaxpr/dot_general | solution.py:24
  462.5 6.9 %fusion.1042 = f32[8,64,256]{2,1,0:T(8,128)S(1)} fusion(f32[8,64,256]{2,1,0:T(8,128)S(1)} %get-tuple-element.798, s32[]{:T(128)} %get-tuple-element.797, f32[64,2048]{1,0:T(8,128)S(1)} %get-tuple-element.817, f32[]{:T(128)} %bitcast.462, f32[256]{0:T(256)S(1)} %bitcast.525, f32[2048]{0:T(1024)S(1)} %bitcast.503, f32[]{:T(128)} %bitcast.466, ...), kind=kOutput, calls=%fused_computation.138.clone.1 | convolution fusion | flops 415236096 | bytes 645148 | tf_op jit(solution)/shard_map/while/body/eval_jaxpr/dot_general | solution.py:24
  471.5 6.9 %fusion.1042 = f32[8,64,256]{2,1,0:T(8,128)S(1)} fusion(f32[8,64,256]{2,1,0:T(8,128)S(1)} %get-tuple-element.798, s32[]{:T(128)} %get-tuple-element.797, f32[64,2048]{1,0:T(8,128)S(1)} %get-tuple-element.817, f32[]{:T(128)} %bitcast.462, f32[256]{0:T(256)S(1)} %bitcast.525, f32[2048]{0:T(1024)S(1)} %bitcast.503, f32[]{:T(128)} %bitcast.466, ...), kind=kOutput, calls=%fused_computation.138.clone.1 | convolution fusion | flops 415236096 | bytes 645148 | tf_op jit(solution)/shard_map/while/body/eval_jaxpr/dot_general | solution.py:24
  480.5 6.9 %fusion.1042 = f32[8,64,256]{2,1,0:T(8,128)S(1)} fusion(f32[8,64,256]{2,1,0:T(8,128)S(1)} %get-tuple-element.798, s32[]{:T(128)} %get-tuple-element.797, f32[64,2048]{1,0:T(8,128)S(1)} %get-tuple-element.817, f32[]{:T(128)} %bitcast.462, f32[256]{0:T(256)S(1)} %bitcast.525, f32[2048]{0:T(1024)S(1)} %bitcast.503, f32[]{:T(128)} %bitcast.466, ...), kind=kOutput, calls=%fused_computation.138.clone.1 | convolution fusion | flops 415236096 | bytes 645148 | tf_op jit(solution)/shard_map/while/body/eval_jaxpr/dot_general | solution.py:24
  489.5 6.9 %fusion.1042 = f32[8,64,256]{2,1,0:T(8,128)S(1)} fusion(f32[8,64,256]{2,1,0:T(8,128)S(1)} %get-tuple-element.798, s32[]{:T(128)} %get-tuple-element.797, f32[64,2048]{1,0:T(8,128)S(1)} %get-tuple-element.817, f32[]{:T(128)} %bitcast.462, f32[256]{0:T(256)S(1)} %bitcast.525, f32[2048]{0:T(1024)S(1)} %bitcast.503, f32[]{:T(128)} %bitcast.466, ...), kind=kOutput, calls=%fused_computation.138.clone.1 | convolution fusion | flops 415236096 | bytes 645148 | tf_op jit(solution)/shard_map/while/body/eval_jaxpr/dot_general | solution.py:24
  498.5 6.9 %fusion.1042 = f32[8,64,256]{2,1,0:T(8,128)S(1)} fusion(f32[8,64,256]{2,1,0:T(8,128)S(1)} %get-tuple-element.798, s32[]{:T(128)} %get-tuple-element.797, f32[64,2048]{1,0:T(8,128)S(1)} %get-tuple-element.817, f32[]{:T(128)} %bitcast.462, f32[256]{0:T(256)S(1)} %bitcast.525, f32[2048]{0:T(1024)S(1)} %bitcast.503, f32[]{:T(128)} %bitcast.466, ...), kind=kOutput, calls=%fused_computation.138.clone.1 | convolution fusion | flops 415236096 | bytes 645148 | tf_op jit(solution)/shard_map/while/body/eval_jaxpr/dot_general | solution.py:24
  507.5 6.9 %fusion.1042 = f32[8,64,256]{2,1,0:T(8,128)S(1)} fusion(f32[8,64,256]{2,1,0:T(8,128)S(1)} %get-tuple-element.798, s32[]{:T(128)} %get-tuple-element.797, f32[64,2048]{1,0:T(8,128)S(1)} %get-tuple-element.817, f32[]{:T(128)} %bitcast.462, f32[256]{0:T(256)S(1)} %bitcast.525, f32[2048]{0:T(1024)S(1)} %bitcast.503, f32[]{:T(128)} %bitcast.466, ...), kind=kOutput, calls=%fused_computation.138.clone.1 | convolution fusion | flops 415236096 | bytes 645148 | tf_op jit(solution)/shard_map/while/body/eval_jaxpr/dot_general | solution.py:24
  516.5 6.9 %fusion.1042 = f32[8,64,256]{2,1,0:T(8,128)S(1)} fusion(f32[8,64,256]{2,1,0:T(8,128)S(1)} %get-tuple-element.798, s32[]{:T(128)} %get-tuple-element.797, f32[64,2048]{1,0:T(8,128)S(1)} %get-tuple-element.817, f32[]{:T(128)} %bitcast.462, f32[256]{0:T(256)S(1)} %bitcast.525, f32[2048]{0:T(1024)S(1)} %bitcast.503, f32[]{:T(128)} %bitcast.466, ...), kind=kOutput, calls=%fused_computation.138.clone.1 | convolution fusion | flops 415236096 | bytes 645148 | tf_op jit(solution)/shard_map/while/body/eval_jaxpr/dot_general | solution.py:24
  550.4 5.5 collective-permute-done.11
  557.4 4.9 fusion.159
  585.3 4.9 fusion.579
  594.7 7.6 %multiply_reduce_fusion = (f32[64]{0:T(128)S(1)}, f32[64,2048]{1,0:T(8,128)S(1)}) fusion(f32[64,2048]{1,0:T(8,128)S(1)} %get-tuple-element.833, f32[64,2048]{1,0:T(8,128)S(1)} %bitcast.487, f32[64,256]{1,0:T(8,128)S(1)} %convolution_add_fusion.6, f32[]{:T(128)} %bitcast.86, f32[256]{0:T(256)S(1)} %bitcast.715, f32[2048]{0:T(1024)S(1)} %bitcast.539, ...), kind=kOutput, calls=%fused_computation.182 | convolution fusion | flops 415891392 | bytes 1693980 | tf_op jit(solution)/shard_map/dot_general | solution.py:24
  602.3 29.5 %psum.47 = f32[64]{0:T(128)S(1)} all-reduce(f32[64]{0:T(128)S(1)} %get-tuple-element.465), channel_id=1, replica_groups=mesh['parts'=2,'leaf'=4,'sub'=4] {'leaf','sub'}, use_global_device_ids=true, to_apply=%region_17.19 | all-reduce | flops 64 | bytes 512 | tf_op jit(solution)/shard_map/psum | solution.py:114
  (404 shorter events, 202.9 us)
Async XLA Ops:
  2.0 442.4 %copy-start.2 = (f32[1,2048]{1,0:T(1,128)}, f32[1,2048]{1,0:T(1,128)S(1)}, u32[]{:S(2)}) copy-start(f32[1,2048]{1,0:T(1,128)S(1)} %get-tuple-element.388) | copy-start | bytes 24580
  2.0 442.4 %copy-start.4 = (f32[1,2048]{1,0:T(1,128)}, f32[1,2048]{1,0:T(1,128)S(1)}, u32[]{:S(2)}) copy-start(f32[1,2048]{1,0:T(1,128)S(1)} %get-tuple-element.389) | copy-start | bytes 24580
  3.8 440.6 %copy-start.13 = (f32[1,256]{1,0:T(1,128)}, f32[1,256]{1,0:T(1,128)S(1)}, u32[]{:S(2)}) copy-start(f32[1,256]{1,0:T(1,128)S(1)} %get-tuple-element.448) | copy-start | bytes 3076
  3.8 440.6 %copy-start.15 = (f32[1,256]{1,0:T(1,128)}, f32[1,256]{1,0:T(1,128)S(1)}, u32[]{:S(2)}) copy-start(f32[1,256]{1,0:T(1,128)S(1)} %get-tuple-element.449) | copy-start | bytes 3076
  3.8 440.6 %copy-start.17 = (f32[1,256]{1,0:T(1,128)}, f32[1,256]{1,0:T(1,128)S(1)}, u32[]{:S(2)}) copy-start(f32[1,256]{1,0:T(1,128)S(1)} %get-tuple-element.450) | copy-start | bytes 3076
  3.8 440.6 %copy-start.19 = (f32[1,256]{1,0:T(1,128)}, f32[1,256]{1,0:T(1,128)S(1)}, u32[]{:S(2)}) copy-start(f32[1,256]{1,0:T(1,128)S(1)} %get-tuple-element.451) | copy-start | bytes 3076
  3.8 440.6 %copy-start.21 = (f32[1,256]{1,0:T(1,128)}, f32[1,256]{1,0:T(1,128)S(1)}, u32[]{:S(2)}) copy-start(f32[1,256]{1,0:T(1,128)S(1)} %get-tuple-element.452) | copy-start | bytes 3076
  3.8 440.6 %copy-start.23 = (f32[1,256]{1,0:T(1,128)}, f32[1,256]{1,0:T(1,128)S(1)}, u32[]{:S(2)}) copy-start(f32[1,256]{1,0:T(1,128)S(1)} %get-tuple-element.453) | copy-start | bytes 3076
  11.6 74.1 %collective-permute-start = (f32[70,256]{1,0:T(8,128)S(1)}, f32[70,256]{1,0:T(8,128)S(1)}, u32[]{:S(2)}, u32[]{:S(2)}) collective-permute-start(f32[70,256]{1,0:T(8,128)S(1)} %pad_maximum_fusion.2), channel_id=1, source_target_pairs={{0,1},{1,0},{2,3},{3,2},{4,5},{5,4},{6,7},{7,6},{8,9},{9,8},{10,11... | collective-permute-start | bytes 215048 | tf_op jit(solution)/shard_map/ppermute | solution.py:10
  12.1 295.0 %copy-start.8 = (pred[256]{0:T(512)(128)(4,1)}, pred[256]{0:T(512)(128)(4,1)S(1)}, u32[]{:S(2)}) copy-start(pred[256]{0:T(512)(128)(4,1)S(1)} %compare_and_fusion.3) | copy-start | bytes 772
  12.1 305.5 %copy-start.6 = (pred[256]{0:T(512)(128)(4,1)}, pred[256]{0:T(512)(128)(4,1)S(1)}, u32[]{:S(2)}) copy-start(pred[256]{0:T(512)(128)(4,1)S(1)} %compare_and_fusion.2) | copy-start | bytes 772
  91.5 5.5 collective-permute-start.1
  102.7 4.4 collective-permute-start.2
  112.8 5.3 collective-permute-start.3
  233.2 72.9 %collective-permute-start.4 = (f32[70,256]{1,0:T(8,128)S(1)}, f32[70,256]{1,0:T(8,128)S(1)}, u32[]{:S(2)}, u32[]{:S(2)}) collective-permute-start(f32[70,256]{1,0:T(8,128)S(1)} %pad_maximum_fusion.1), channel_id=1, source_target_pairs={{0,1},{1,0},{2,3},{3,2},{4,5},{5,4},{6,7},{7,6},{8,9},{9,8},{10,11... | collective-permute-start | bytes 215048 | tf_op jit(solution)/shard_map/ppermute | solution.py:10
  311.8 4.7 collective-permute-start.5
  322.3 4.4 collective-permute-start.6
  332.5 5.5 collective-permute-start.7
  451.3 72.4 %collective-permute-start.8 = (f32[70,256]{1,0:T(8,128)S(1)}, f32[70,256]{1,0:T(8,128)S(1)}, u32[]{:S(2)}, u32[]{:S(2)}) collective-permute-start(f32[70,256]{1,0:T(8,128)S(1)} %pad_maximum_fusion), channel_id=1, source_target_pairs={{0,1},{1,0},{2,3},{3,2},{4,5},{5,4},{6,7},{7,6},{8,9},{9,8},{10,11... | collective-permute-start | bytes 215048 | tf_op jit(solution)/shard_map/ppermute | solution.py:10
  529.5 5.8 copy-start.7
  529.5 4.7 collective-permute-start.9
  540.1 4.4 collective-permute-start.10
  550.3 5.5 collective-permute-start.11
  566.6 4.9 copy-start.32
  566.6 4.9 copy-start.34
  566.6 4.9 copy-start.36
  566.6 4.9 copy-start.38
  566.6 4.9 copy-start.40
  575.9 4.9 copy-start.43
  575.9 4.9 copy-start.44
  575.9 4.9 copy-start.45
  575.9 4.9 copy-start.46
  575.9 4.9 copy-start.47
  575.9 4.9 copy-start.48
  585.2 5.0 copy-start.14
  585.2 5.0 copy-start.16
  585.2 5.0 copy-start.18
  585.2 5.0 copy-start.20
  585.2 5.0 copy-start.22
  585.2 5.0 copy-start.24
  585.2 5.0 copy-start.25
  585.2 5.0 copy-start.26
  585.2 5.0 copy-start.27
  585.3 5.0 copy-start.28
  585.3 5.0 copy-start.29
  585.3 5.0 copy-start.30
  594.6 37.2 %copy-start.51 = (f32[64]{0:T(128)S(1)}, f32[64]{0:T(128)}, u32[]{:S(2)}) copy-start(f32[64]{0:T(128)} %copy-done.50) | copy-start | bytes 772
  594.6 37.2 %copy-start.12 = (f32[64]{0:T(128)S(1)}, f32[64]{0:T(128)}, u32[]{:S(2)}) copy-start(f32[64]{0:T(128)} %copy-done.11) | copy-start | bytes 772
  (16 other events, 54.3 us)
where the time goes:
time: 643 us; the launch traced here: 633 us
  matrix products  362 us (56%)
  blocking collectives  150 us (23%)
  local copies, waits for them, and re-layouts  53.5 us (8%)
  waiting for transfers between devices  35.5 us (6%)
  loops' own time  17.4 us (3%)
  starting transfers between devices  8.43 us (1%)
    dot_general x63, matrix products, product(): jnp.dot(first, second, precision=lax.Precision.HIGHEST, preferred_element...  362 us
    psum x2, blocking collectives, body(): curve = lax.psum(jnp.sum(direction * image, axis=1), ('leaf', 'sub'))  59 us
    psum x2, blocking collectives, body(): norm_next = lax.psum(jnp.sum(residual * residual, axis=1), ('leaf', 'sub'))  59 us
    ppermute x12, waiting for transfers between devices, from_partner(): lax.ppermute(shard, axis, [(i, i ^ 1 << stride) for i in range(lax.axis_s...  35.5 us
    psum x1, blocking collectives, body(): norm_now = lax.psum(jnp.sum(residual * residual, axis=1), ('leaf', 'sub'))  31.9 us
    another operation x3, loops' own time, body(): pieces = lax.map(one_block, jnp.arange(blocks))  17.4 us
    slice x25, local copies, waits for them, and re-layouts, kernel(): inverse_scale[axis_number]  16.8 us
    dynamic_slice x24, local copies, waits for them, and re-layouts, body(): pieces = lax.map(one_block, jnp.arange(blocks))  15.3 us
  transfers between devices with their start and end apart: 12, of which 9 were waited for; matrix products, arithmetic and copies ran while one was open for 32% of the time, Pallas kernels for 0%

commit v1 on v0

--- a/solution.py
+++ b/solution.py
@@ -116,7 +116,8 @@
         solution = solution + step_size[:, None] * direction
         residual = residual - step_size[:, None] * image
         if iteration + 1 < ITERS:
-            norm_next = lax.psum(jnp.sum(residual * residual, axis=1), ("leaf", "sub"))
+            row_data = jnp.sum(residual * residual, axis=1)
+            norm_next = lax.psum(lax.psum(row_data, "sub"), "leaf")
         if iteration + 1 < ITERS:
             direction = residual + (norm_next / norm_now)[:, None] * direction
             norm_now = norm_next

time: 643 us -> 611 us (0.950)
  blocking collectives: 150 us -> 120 us
  waiting for transfers between devices: 35.5 us -> 28.1 us
  starting transfers between devices: 8.43 us -> 15.4 us
    psum x2 -> x4, blocking collectives: 59 us -> 28.2 us  [body(): norm_next = lax.psum(lax.psum(row_data, 'sub'), 'leaf')]
    ppermute x12, waiting for transfers between devices: 35.5 us -> 28.1 us  [from_partner(): lax.ppermute(shard, axis, [(i, i ^ 1 << stride) for i in range(lax.axis_s...]
    ppermute x12, starting transfers between devices: 8.43 us -> 15.4 us  [from_partner(): lax.ppermute(shard, axis, [(i, i ^ 1 << stride) for i in range(lax.axis_s...]
  transfers between devices with their start and end apart: 12 -> 12, of which waited for: 9 -> 9; matrix products, arithmetic and copies ran while one was open for 32% -> 34% of each run, Pallas kernels for 0% -> 0%
where the time goes in v1:
time: 611 us; the launch traced here: 602 us
  matrix products  364 us (60%)
  blocking collectives  120 us (20%)
  local copies, waits for them, and re-layouts  52.2 us (9%)
  waiting for transfers between devices  28.1 us (5%)
  starting transfers between devices  15.4 us (3%)
  loops' own time  15.4 us (3%)
    dot_general x63, matrix products, product(): jnp.dot(first, second, precision=lax.Precision.HIGHEST, preferred_element...  364 us
    psum x2, blocking collectives, body(): curve = lax.psum(jnp.sum(direction * image, axis=1), ('leaf', 'sub'))  59.6 us
    psum x1, blocking collectives, body(): norm_now = lax.psum(jnp.sum(residual * residual, axis=1), ('leaf', 'sub'))  31.9 us
    psum x4, blocking collectives, body(): norm_next = lax.psum(lax.psum(row_data, 'sub'), 'leaf')  28.2 us
    ppermute x12, waiting for transfers between devices, from_partner(): lax.ppermute(shard, axis, [(i, i ^ 1 << stride) for i in range(lax.axis_s...  28.1 us
    slice x25, local copies, waits for them, and re-layouts, kernel(): inverse_scale[axis_number]  16.6 us
    another operation x3, loops' own time, body(): pieces = lax.map(one_block, jnp.arange(blocks))  15.4 us
    ppermute x12, starting transfers between devices, from_partner(): lax.ppermute(shard, axis, [(i, i ^ 1 << stride) for i in range(lax.axis_s...  15.4 us
  transfers between devices with their start and end apart: 12, of which 9 were waited for; matrix products, arithmetic and copies ran while one was open for 34% of the time, Pallas kernels for 0%

profile of v1, /device:TPU:0, one launch (start us, length us, event | category | flops | bytes accessed | tf_op | source)
XLA Modules:
  0.0 601.9 jit_solution(18124605497020648596)
XLA Ops:
  4.5 7.0 %convolution_bitcast_fusion = f32[64,256]{1,0:T(8,128)S(1)} fusion(f32[64,2048]{1,0:T(8,128)S(1)} %copy-done.1, f32[]{:T(128)} %bitcast.86, f32[256]{0:T(256)S(1)} %bitcast.707, f32[2048]{0:T(1024)S(1)} %bitcast.534, f32[]{:T(128)} %bitcast.83, f32[256]{0:T(256)S(1)} %bitcast.716, f32[2048]{0:T(1024)S(1)} %bitcast.540, f32[]{:T(128)} %bitcast.80, ...), kind=kOutput, calls=%fused_computation.179 | convolution fusion | flops 415236096 | bytes 645144 | tf_op jit(solution)/shard_map/dot_general | solution.py:24
  12.3 72.0 %while.30 = (s32[]{:T(128)}, f32[8,64,256]{2,1,0:T(8,128)S(1)}, f32[6,2048]{1,0:T(8,128)S(1)}, s32[8]{0:T(128)S(1)}, f32[6]{0:T(128)S(1)}, /*index=5*/f32[64,204...) while((s32[]{:T(128)}, f32[8,64,256]{2,1,0:T(8,128)S(1)}, ...), condition=%wide.region_3.4_spmd, body=%wide.region_2.3_spmd.sunk | while | flops 415236096 | bytes 756071 | solution.py:110
  14.2 7.0 %fusion.1032 = f32[8,64,256]{2,1,0:T(8,128)S(1)} fusion(f32[8,64,256]{2,1,0:T(8,128)S(1)} %get-tuple-element.708, s32[]{:T(128)} %get-tuple-element.707, f32[64,2048]{1,0:T(8,128)S(1)} %get-tuple-element.727, f32[]{:T(128)} %bitcast.420, f32[256]{0:T(256)S(1)} %bitcast.513, f32[2048]{0:T(1024)S(1)} %bitcast.491, f32[]{:T(128)} %bitcast.424, ...), kind=kOutput, calls=%fused_computation.40.clone.1 | convolution fusion | flops 415236096 | bytes 645148 | tf_op jit(solution)/shard_map/while/body/eval_jaxpr/dot_general | solution.py:24
  23.2 7.0 %fusion.1032 = f32[8,64,256]{2,1,0:T(8,128)S(1)} fusion(f32[8,64,256]{2,1,0:T(8,128)S(1)} %get-tuple-element.708, s32[]{:T(128)} %get-tuple-element.707, f32[64,2048]{1,0:T(8,128)S(1)} %get-tuple-element.727, f32[]{:T(128)} %bitcast.420, f32[256]{0:T(256)S(1)} %bitcast.513, f32[2048]{0:T(1024)S(1)} %bitcast.491, f32[]{:T(128)} %bitcast.424, ...), kind=kOutput, calls=%fused_computation.40.clone.1 | convolution fusion | flops 415236096 | bytes 645148 | tf_op jit(solution)/shard_map/while/body/eval_jaxpr/dot_general | solution.py:24
  32.2 7.0 %fusion.1032 = f32[8,64,256]{2,1,0:T(8,128)S(1)} fusion(f32[8,64,256]{2,1,0:T(8,128)S(1)} %get-tuple-element.708, s32[]{:T(128)} %get-tuple-element.707, f32[64,2048]{1,0:T(8,128)S(1)} %get-tuple-element.727, f32[]{:T(128)} %bitcast.420, f32[256]{0:T(256)S(1)} %bitcast.513, f32[2048]{0:T(1024)S(1)} %bitcast.491, f32[]{:T(128)} %bitcast.424, ...), kind=kOutput, calls=%fused_computation.40.clone.1 | convolution fusion | flops 415236096 | bytes 645148 | tf_op jit(solution)/shard_map/while/body/eval_jaxpr/dot_general | solution.py:24
  41.1 7.0 %fusion.1032 = f32[8,64,256]{2,1,0:T(8,128)S(1)} fusion(f32[8,64,256]{2,1,0:T(8,128)S(1)} %get-tuple-element.708, s32[]{:T(128)} %get-tuple-element.707, f32[64,2048]{1,0:T(8,128)S(1)} %get-tuple-element.727, f32[]{:T(128)} %bitcast.420, f32[256]{0:T(256)S(1)} %bitcast.513, f32[2048]{0:T(1024)S(1)} %bitcast.491, f32[]{:T(128)} %bitcast.424, ...), kind=kOutput, calls=%fused_computation.40.clone.1 | convolution fusion | flops 415236096 | bytes 645148 | tf_op jit(solution)/shard_map/while/body/eval_jaxpr/dot_general | solution.py:24
  50.1 7.0 %fusion.1032 = f32[8,64,256]{2,1,0:T(8,128)S(1)} fusion(f32[8,64,256]{2,1,0:T(8,128)S(1)} %get-tuple-element.708, s32[]{:T(128)} %get-tuple-element.707, f32[64,2048]{1,0:T(8,128)S(1)} %get-tuple-element.727, f32[]{:T(128)} %bitcast.420, f32[256]{0:T(256)S(1)} %bitcast.513, f32[2048]{0:T(1024)S(1)} %bitcast.491, f32[]{:T(128)} %bitcast.424, ...), kind=kOutput, calls=%fused_computation.40.clone.1 | convolution fusion | flops 415236096 | bytes 645148 | tf_op jit(solution)/shard_map/while/body/eval_jaxpr/dot_general | solution.py:24
  59.1 7.0 %fusion.1032 = f32[8,64,256]{2,1,0:T(8,128)S(1)} fusion(f32[8,64,256]{2,1,0:T(8,128)S(1)} %get-tuple-element.708, s32[]{:T(128)} %get-tuple-element.707, f32[64,2048]{1,0:T(8,128)S(1)} %get-tuple-element.727, f32[]{:T(128)} %bitcast.420, f32[256]{0:T(256)S(1)} %bitcast.513, f32[2048]{0:T(1024)S(1)} %bitcast.491, f32[]{:T(128)} %bitcast.424, ...), kind=kOutput, calls=%fused_computation.40.clone.1 | convolution fusion | flops 415236096 | bytes 645148 | tf_op jit(solution)/shard_map/while/body/eval_jaxpr/dot_general | solution.py:24
  68.0 7.0 %fusion.1032 = f32[8,64,256]{2,1,0:T(8,128)S(1)} fusion(f32[8,64,256]{2,1,0:T(8,128)S(1)} %get-tuple-element.708, s32[]{:T(128)} %get-tuple-element.707, f32[64,2048]{1,0:T(8,128)S(1)} %get-tuple-element.727, f32[]{:T(128)} %bitcast.420, f32[256]{0:T(256)S(1)} %bitcast.513, f32[2048]{0:T(1024)S(1)} %bitcast.491, f32[]{:T(128)} %bitcast.424, ...), kind=kOutput, calls=%fused_computation.40.clone.1 | convolution fusion | flops 415236096 | bytes 645148 | tf_op jit(solution)/shard_map/while/body/eval_jaxpr/dot_general | solution.py:24
  77.0 7.0 %fusion.1032 = f32[8,64,256]{2,1,0:T(8,128)S(1)} fusion(f32[8,64,256]{2,1,0:T(8,128)S(1)} %get-tuple-element.708, s32[]{:T(128)} %get-tuple-element.707, f32[64,2048]{1,0:T(8,128)S(1)} %get-tuple-element.727, f32[]{:T(128)} %bitcast.420, f32[256]{0:T(256)S(1)} %bitcast.513, f32[2048]{0:T(1024)S(1)} %bitcast.491, f32[]{:T(128)} %bitcast.424, ...), kind=kOutput, calls=%fused_computation.40.clone.1 | convolution fusion | flops 415236096 | bytes 645148 | tf_op jit(solution)/shard_map/while/body/eval_jaxpr/dot_general | solution.py:24
  118.9 4.9 fusion.211
  137.4 4.9 fusion.569
  155.8 8.1 %multiply_reduce_fusion.4 = (f32[64]{0:T(128)S(1)}, f32[64]{0:T(128)S(1)}, f32[64,2048]{1,0:T(8,128)S(1)}) fusion(f32[64,2048]{1,0:T(8,128)S(1)} %get-tuple-element.829, f32[64,2048]{1,0:T(8,128)S(1)} %bitcast.488, f32[64,256]{1,0:T(8,128)S(1)} %convolution_add_fusion.14, f32[]{:T(128)} %bitcast.86, f32[256]{0:T(256)S(1)} %bitcast.709, ...), kind=kOutput, calls=%fused_computation.248 | convolution fusion | flops 416153472 | bytes 1694236 | tf_op jit(solution)/shard_map/dot_general | solution.py:24
  163.8 31.9 %all-reduce = (f32[64]{0:T(128)S(1)}, f32[64]{0:T(128)S(1)}) all-reduce(f32[64]{0:T(128)S(1)} %get-tuple-element.103, f32[64]{0:T(128)S(1)} %get-tuple-element.102), channel_id=1, replica_groups=mesh['parts'=2,'leaf'=4,'sub'=4] {'leaf','sub'}, use_global_device_ids=true, to_apply=%region_1.2 | all-reduce | flops 128 | bytes 1024 | tf_op jit(solution)/shard_map/psum | solution.py:70
  196.0 5.8 psum.58
  201.8 8.4 %psum.59 = f32[64]{0:T(128)S(1)} all-reduce(f32[64]{0:T(128)S(1)} %psum.58), channel_id=1, replica_groups=mesh['parts'=2,'leaf'=4,'sub'=4] {'leaf'}, use_global_device_ids=true, to_apply=%region_8.10 | all-reduce | flops 64 | bytes 512 | tf_op jit(solution)/shard_map/psum | solution.py:120
  210.3 6.8 %fusion.964 = f32[64,256]{1,0:T(8,128)S(1)} fusion(f32[64,2048]{1,0:T(8,128)S(1)} %multiply_add_fusion.2, f32[]{:T(128)} %bitcast.86, f32[256]{0:T(256)S(1)} %bitcast.710, f32[2048]{0:T(1024)S(1)} %bitcast.536, f32[]{:T(128)} %bitcast.83, f32[256]{0:T(256)S(1)} %bitcast.719, f32[2048]{0:T(1024)S(1)} %bitcast.542, f32[]{:T(128)} %bitcast.80, ...), kind=kOutput, calls=%fused_computation.1244 | convolution fusion | flops 415236096 | bytes 645144 | tf_op jit(solution)/shard_map/dot_general | solution.py:24
  217.3 71.9 %while.31 = (s32[]{:T(128)}, f32[8,64,256]{2,1,0:T(8,128)S(1)}, f32[6,2048]{1,0:T(8,128)S(1)}, s32[8]{0:T(128)S(1)}, f32[6]{0:T(128)S(1)}, /*index=5*/f32[64,204...) while((s32[]{:T(128)}, f32[8,64,256]{2,1,0:T(8,128)S(1)}, ...), condition=%wide.region_10.12_spmd, body=%wide.region_9.11_spmd.sunk | while | flops 415236096 | bytes 756071 | solution.py:110
  219.2 7.0 %fusion.1037 = f32[8,64,256]{2,1,0:T(8,128)S(1)} fusion(f32[8,64,256]{2,1,0:T(8,128)S(1)} %get-tuple-element.753, s32[]{:T(128)} %get-tuple-element.752, f32[64,2048]{1,0:T(8,128)S(1)} %get-tuple-element.772, f32[]{:T(128)} %bitcast.441, f32[256]{0:T(256)S(1)} %bitcast.519, f32[2048]{0:T(1024)S(1)} %bitcast.497, f32[]{:T(128)} %bitcast.445, ...), kind=kOutput, calls=%fused_computation.89.clone.1 | convolution fusion | flops 415236096 | bytes 645148 | tf_op jit(solution)/shard_map/while/body/eval_jaxpr/dot_general | solution.py:24
  228.2 7.0 %fusion.1037 = f32[8,64,256]{2,1,0:T(8,128)S(1)} fusion(f32[8,64,256]{2,1,0:T(8,128)S(1)} %get-tuple-element.753, s32[]{:T(128)} %get-tuple-element.752, f32[64,2048]{1,0:T(8,128)S(1)} %get-tuple-element.772, f32[]{:T(128)} %bitcast.441, f32[256]{0:T(256)S(1)} %bitcast.519, f32[2048]{0:T(1024)S(1)} %bitcast.497, f32[]{:T(128)} %bitcast.445, ...), kind=kOutput, calls=%fused_computation.89.clone.1 | convolution fusion | flops 415236096 | bytes 645148 | tf_op jit(solution)/shard_map/while/body/eval_jaxpr/dot_general | solution.py:24
  237.2 7.0 %fusion.1037 = f32[8,64,256]{2,1,0:T(8,128)S(1)} fusion(f32[8,64,256]{2,1,0:T(8,128)S(1)} %get-tuple-element.753, s32[]{:T(128)} %get-tuple-element.752, f32[64,2048]{1,0:T(8,128)S(1)} %get-tuple-element.772, f32[]{:T(128)} %bitcast.441, f32[256]{0:T(256)S(1)} %bitcast.519, f32[2048]{0:T(1024)S(1)} %bitcast.497, f32[]{:T(128)} %bitcast.445, ...), kind=kOutput, calls=%fused_computation.89.clone.1 | convolution fusion | flops 415236096 | bytes 645148 | tf_op jit(solution)/shard_map/while/body/eval_jaxpr/dot_general | solution.py:24
  246.1 7.0 %fusion.1037 = f32[8,64,256]{2,1,0:T(8,128)S(1)} fusion(f32[8,64,256]{2,1,0:T(8,128)S(1)} %get-tuple-element.753, s32[]{:T(128)} %get-tuple-element.752, f32[64,2048]{1,0:T(8,128)S(1)} %get-tuple-element.772, f32[]{:T(128)} %bitcast.441, f32[256]{0:T(256)S(1)} %bitcast.519, f32[2048]{0:T(1024)S(1)} %bitcast.497, f32[]{:T(128)} %bitcast.445, ...), kind=kOutput, calls=%fused_computation.89.clone.1 | convolution fusion | flops 415236096 | bytes 645148 | tf_op jit(solution)/shard_map/while/body/eval_jaxpr/dot_general | solution.py:24
  255.1 7.0 %fusion.1037 = f32[8,64,256]{2,1,0:T(8,128)S(1)} fusion(f32[8,64,256]{2,1,0:T(8,128)S(1)} %get-tuple-element.753, s32[]{:T(128)} %get-tuple-element.752, f32[64,2048]{1,0:T(8,128)S(1)} %get-tuple-element.772, f32[]{:T(128)} %bitcast.441, f32[256]{0:T(256)S(1)} %bitcast.519, f32[2048]{0:T(1024)S(1)} %bitcast.497, f32[]{:T(128)} %bitcast.445, ...), kind=kOutput, calls=%fused_computation.89.clone.1 | convolution fusion | flops 415236096 | bytes 645148 | tf_op jit(solution)/shard_map/while/body/eval_jaxpr/dot_general | solution.py:24
  264.1 7.0 %fusion.1037 = f32[8,64,256]{2,1,0:T(8,128)S(1)} fusion(f32[8,64,256]{2,1,0:T(8,128)S(1)} %get-tuple-element.753, s32[]{:T(128)} %get-tuple-element.752, f32[64,2048]{1,0:T(8,128)S(1)} %get-tuple-element.772, f32[]{:T(128)} %bitcast.441, f32[256]{0:T(256)S(1)} %bitcast.519, f32[2048]{0:T(1024)S(1)} %bitcast.497, f32[]{:T(128)} %bitcast.445, ...), kind=kOutput, calls=%fused_computation.89.clone.1 | convolution fusion | flops 415236096 | bytes 645148 | tf_op jit(solution)/shard_map/while/body/eval_jaxpr/dot_general | solution.py:24
  273.0 7.0 %fusion.1037 = f32[8,64,256]{2,1,0:T(8,128)S(1)} fusion(f32[8,64,256]{2,1,0:T(8,128)S(1)} %get-tuple-element.753, s32[]{:T(128)} %get-tuple-element.752, f32[64,2048]{1,0:T(8,128)S(1)} %get-tuple-element.772, f32[]{:T(128)} %bitcast.441, f32[256]{0:T(256)S(1)} %bitcast.519, f32[2048]{0:T(1024)S(1)} %bitcast.497, f32[]{:T(128)} %bitcast.445, ...), kind=kOutput, calls=%fused_computation.89.clone.1 | convolution fusion | flops 415236096 | bytes 645148 | tf_op jit(solution)/shard_map/while/body/eval_jaxpr/dot_general | solution.py:24
  282.0 7.0 %fusion.1037 = f32[8,64,256]{2,1,0:T(8,128)S(1)} fusion(f32[8,64,256]{2,1,0:T(8,128)S(1)} %get-tuple-element.753, s32[]{:T(128)} %get-tuple-element.752, f32[64,2048]{1,0:T(8,128)S(1)} %get-tuple-element.772, f32[]{:T(128)} %bitcast.441, f32[256]{0:T(256)S(1)} %bitcast.519, f32[2048]{0:T(1024)S(1)} %bitcast.497, f32[]{:T(128)} %bitcast.445, ...), kind=kOutput, calls=%fused_computation.89.clone.1 | convolution fusion | flops 415236096 | bytes 645148 | tf_op jit(solution)/shard_map/while/body/eval_jaxpr/dot_general | solution.py:24
  322.5 4.9 fusion.185
  331.8 4.9 fusion.577
  341.0 4.9 fusion.575
  359.4 7.9 %multiply_reduce_fusion.2 = (f32[64]{0:T(128)S(1)}, f32[64,2048]{1,0:T(8,128)S(1)}) fusion(f32[64,2048]{1,0:T(8,128)S(1)} %get-tuple-element.832, f32[64,2048]{1,0:T(8,128)S(1)} %bitcast.489, f32[64,256]{1,0:T(8,128)S(1)} %convolution_add_fusion.10, f32[]{:T(128)} %bitcast.86, f32[256]{0:T(256)S(1)} %bitcast.712, f32[2048]{0:T(1024)S(1)} %bitcast.537, ...), kind=kOutput, calls=%fused_computation.215 | convolution fusion | flops 415891392 | bytes 1693980 | tf_op jit(solution)/shard_map/dot_general | solution.py:24
  367.2 29.5 %psum.60 = f32[64]{0:T(128)S(1)} all-reduce(f32[64]{0:T(128)S(1)} %get-tuple-element.463), channel_id=1, replica_groups=mesh['parts'=2,'leaf'=4,'sub'=4] {'leaf','sub'}, use_global_device_ids=true, to_apply=%region_12.14 | all-reduce | flops 64 | bytes 512 | tf_op jit(solution)/shard_map/psum | solution.py:114
  397.3 5.7 psum.61
  403.0 8.4 %psum.62 = f32[64]{0:T(128)S(1)} all-reduce(f32[64]{0:T(128)S(1)} %psum.61), channel_id=1, replica_groups=mesh['parts'=2,'leaf'=4,'sub'=4] {'leaf'}, use_global_device_ids=true, to_apply=%region_15.17 | all-reduce | flops 64 | bytes 512 | tf_op jit(solution)/shard_map/psum | solution.py:120
  412.1 6.8 %fusion.963 = f32[64,256]{1,0:T(8,128)S(1)} fusion(f32[64,2048]{1,0:T(8,128)S(1)} %multiply_add_fusion.1, f32[]{:T(128)} %bitcast.86, f32[256]{0:T(256)S(1)} %bitcast.713, f32[2048]{0:T(1024)S(1)} %bitcast.538, f32[]{:T(128)} %bitcast.83, f32[256]{0:T(256)S(1)} %bitcast.722, f32[2048]{0:T(1024)S(1)} %bitcast.544, f32[]{:T(128)} %bitcast.80, ...), kind=kOutput, calls=%fused_computation.1243 | convolution fusion | flops 415236096 | bytes 645144 | tf_op jit(solution)/shard_map/dot_general | solution.py:24
  419.1 72.5 %while.32 = (s32[]{:T(128)}, f32[8,64,256]{2,1,0:T(8,128)S(1)}, f32[6,2048]{1,0:T(8,128)S(1)}, s32[8]{0:T(128)S(1)}, f32[6]{0:T(128)S(1)}, /*index=5*/f32[64,204...) while((s32[]{:T(128)}, f32[8,64,256]{2,1,0:T(8,128)S(1)}, ...), condition=%wide.region_17.19_spmd, body=%wide.region_16.18_spmd.sunk | while | flops 415236096 | bytes 756071 | solution.py:110
  421.2 7.0 %fusion.1042 = f32[8,64,256]{2,1,0:T(8,128)S(1)} fusion(f32[8,64,256]{2,1,0:T(8,128)S(1)} %get-tuple-element.798, s32[]{:T(128)} %get-tuple-element.797, f32[64,2048]{1,0:T(8,128)S(1)} %get-tuple-element.817, f32[]{:T(128)} %bitcast.462, f32[256]{0:T(256)S(1)} %bitcast.525, f32[2048]{0:T(1024)S(1)} %bitcast.503, f32[]{:T(128)} %bitcast.466, ...), kind=kOutput, calls=%fused_computation.138.clone.1 | convolution fusion | flops 415236096 | bytes 645148 | tf_op jit(solution)/shard_map/while/body/eval_jaxpr/dot_general | solution.py:24
  430.2 6.9 %fusion.1042 = f32[8,64,256]{2,1,0:T(8,128)S(1)} fusion(f32[8,64,256]{2,1,0:T(8,128)S(1)} %get-tuple-element.798, s32[]{:T(128)} %get-tuple-element.797, f32[64,2048]{1,0:T(8,128)S(1)} %get-tuple-element.817, f32[]{:T(128)} %bitcast.462, f32[256]{0:T(256)S(1)} %bitcast.525, f32[2048]{0:T(1024)S(1)} %bitcast.503, f32[]{:T(128)} %bitcast.466, ...), kind=kOutput, calls=%fused_computation.138.clone.1 | convolution fusion | flops 415236096 | bytes 645148 | tf_op jit(solution)/shard_map/while/body/eval_jaxpr/dot_general | solution.py:24
  439.2 7.0 %fusion.1042 = f32[8,64,256]{2,1,0:T(8,128)S(1)} fusion(f32[8,64,256]{2,1,0:T(8,128)S(1)} %get-tuple-element.798, s32[]{:T(128)} %get-tuple-element.797, f32[64,2048]{1,0:T(8,128)S(1)} %get-tuple-element.817, f32[]{:T(128)} %bitcast.462, f32[256]{0:T(256)S(1)} %bitcast.525, f32[2048]{0:T(1024)S(1)} %bitcast.503, f32[]{:T(128)} %bitcast.466, ...), kind=kOutput, calls=%fused_computation.138.clone.1 | convolution fusion | flops 415236096 | bytes 645148 | tf_op jit(solution)/shard_map/while/body/eval_jaxpr/dot_general | solution.py:24
  448.3 7.0 %fusion.1042 = f32[8,64,256]{2,1,0:T(8,128)S(1)} fusion(f32[8,64,256]{2,1,0:T(8,128)S(1)} %get-tuple-element.798, s32[]{:T(128)} %get-tuple-element.797, f32[64,2048]{1,0:T(8,128)S(1)} %get-tuple-element.817, f32[]{:T(128)} %bitcast.462, f32[256]{0:T(256)S(1)} %bitcast.525, f32[2048]{0:T(1024)S(1)} %bitcast.503, f32[]{:T(128)} %bitcast.466, ...), kind=kOutput, calls=%fused_computation.138.clone.1 | convolution fusion | flops 415236096 | bytes 645148 | tf_op jit(solution)/shard_map/while/body/eval_jaxpr/dot_general | solution.py:24
  457.3 6.9 %fusion.1042 = f32[8,64,256]{2,1,0:T(8,128)S(1)} fusion(f32[8,64,256]{2,1,0:T(8,128)S(1)} %get-tuple-element.798, s32[]{:T(128)} %get-tuple-element.797, f32[64,2048]{1,0:T(8,128)S(1)} %get-tuple-element.817, f32[]{:T(128)} %bitcast.462, f32[256]{0:T(256)S(1)} %bitcast.525, f32[2048]{0:T(1024)S(1)} %bitcast.503, f32[]{:T(128)} %bitcast.466, ...), kind=kOutput, calls=%fused_computation.138.clone.1 | convolution fusion | flops 415236096 | bytes 645148 | tf_op jit(solution)/shard_map/while/body/eval_jaxpr/dot_general | solution.py:24
  466.3 7.0 %fusion.1042 = f32[8,64,256]{2,1,0:T(8,128)S(1)} fusion(f32[8,64,256]{2,1,0:T(8,128)S(1)} %get-tuple-element.798, s32[]{:T(128)} %get-tuple-element.797, f32[64,2048]{1,0:T(8,128)S(1)} %get-tuple-element.817, f32[]{:T(128)} %bitcast.462, f32[256]{0:T(256)S(1)} %bitcast.525, f32[2048]{0:T(1024)S(1)} %bitcast.503, f32[]{:T(128)} %bitcast.466, ...), kind=kOutput, calls=%fused_computation.138.clone.1 | convolution fusion | flops 415236096 | bytes 645148 | tf_op jit(solution)/shard_map/while/body/eval_jaxpr/dot_general | solution.py:24
  475.4 7.0 %fusion.1042 = f32[8,64,256]{2,1,0:T(8,128)S(1)} fusion(f32[8,64,256]{2,1,0:T(8,128)S(1)} %get-tuple-element.798, s32[]{:T(128)} %get-tuple-element.797, f32[64,2048]{1,0:T(8,128)S(1)} %get-tuple-element.817, f32[]{:T(128)} %bitcast.462, f32[256]{0:T(256)S(1)} %bitcast.525, f32[2048]{0:T(1024)S(1)} %bitcast.503, f32[]{:T(128)} %bitcast.466, ...), kind=kOutput, calls=%fused_computation.138.clone.1 | convolution fusion | flops 415236096 | bytes 645148 | tf_op jit(solution)/shard_map/while/body/eval_jaxpr/dot_general | solution.py:24
  484.4 6.9 %fusion.1042 = f32[8,64,256]{2,1,0:T(8,128)S(1)} fusion(f32[8,64,256]{2,1,0:T(8,128)S(1)} %get-tuple-element.798, s32[]{:T(128)} %get-tuple-element.797, f32[64,2048]{1,0:T(8,128)S(1)} %get-tuple-element.817, f32[]{:T(128)} %bitcast.462, f32[256]{0:T(256)S(1)} %bitcast.525, f32[2048]{0:T(1024)S(1)} %bitcast.503, f32[]{:T(128)} %bitcast.466, ...), kind=kOutput, calls=%fused_computation.138.clone.1 | convolution fusion | flops 415236096 | bytes 645148 | tf_op jit(solution)/shard_map/while/body/eval_jaxpr/dot_general | solution.py:24
  525.1 4.9 fusion.159
  543.7 4.9 fusion.581
  553.1 4.9 fusion.579
  562.4 7.7 %multiply_reduce_fusion = (f32[64]{0:T(128)S(1)}, f32[64,2048]{1,0:T(8,128)S(1)}) fusion(f32[64,2048]{1,0:T(8,128)S(1)} %get-tuple-element.833, f32[64,2048]{1,0:T(8,128)S(1)} %bitcast.487, f32[64,256]{1,0:T(8,128)S(1)} %convolution_add_fusion.6, f32[]{:T(128)} %bitcast.86, f32[256]{0:T(256)S(1)} %bitcast.715, f32[2048]{0:T(1024)S(1)} %bitcast.539, ...), kind=kOutput, calls=%fused_computation.182 | convolution fusion | flops 415891392 | bytes 1693980 | tf_op jit(solution)/shard_map/dot_general | solution.py:24
  570.1 30.1 %psum.63 = f32[64]{0:T(128)S(1)} all-reduce(f32[64]{0:T(128)S(1)} %get-tuple-element.465), channel_id=1, replica_groups=mesh['parts'=2,'leaf'=4,'sub'=4] {'leaf','sub'}, use_global_device_ids=true, to_apply=%region_19.21 | all-reduce | flops 64 | bytes 512 | tf_op jit(solution)/shard_map/psum | solution.py:114
  (406 shorter events, 212.3 us)
Async XLA Ops:
  2.0 410.1 %copy-start.2 = (f32[1,2048]{1,0:T(1,128)}, f32[1,2048]{1,0:T(1,128)S(1)}, u32[]{:S(2)}) copy-start(f32[1,2048]{1,0:T(1,128)S(1)} %get-tuple-element.388) | copy-start | bytes 24580
  2.0 410.1 %copy-start.4 = (f32[1,2048]{1,0:T(1,128)}, f32[1,2048]{1,0:T(1,128)S(1)}, u32[]{:S(2)}) copy-start(f32[1,2048]{1,0:T(1,128)S(1)} %get-tuple-element.389) | copy-start | bytes 24580
  3.8 408.3 %copy-start.13 = (f32[1,256]{1,0:T(1,128)}, f32[1,256]{1,0:T(1,128)S(1)}, u32[]{:S(2)}) copy-start(f32[1,256]{1,0:T(1,128)S(1)} %get-tuple-element.448) | copy-start | bytes 3076
  3.8 408.3 %copy-start.15 = (f32[1,256]{1,0:T(1,128)}, f32[1,256]{1,0:T(1,128)S(1)}, u32[]{:S(2)}) copy-start(f32[1,256]{1,0:T(1,128)S(1)} %get-tuple-element.449) | copy-start | bytes 3076
  3.8 408.3 %copy-start.17 = (f32[1,256]{1,0:T(1,128)}, f32[1,256]{1,0:T(1,128)S(1)}, u32[]{:S(2)}) copy-start(f32[1,256]{1,0:T(1,128)S(1)} %get-tuple-element.450) | copy-start | bytes 3076
  3.8 408.3 %copy-start.19 = (f32[1,256]{1,0:T(1,128)}, f32[1,256]{1,0:T(1,128)S(1)}, u32[]{:S(2)}) copy-start(f32[1,256]{1,0:T(1,128)S(1)} %get-tuple-element.451) | copy-start | bytes 3076
  3.8 408.3 %copy-start.21 = (f32[1,256]{1,0:T(1,128)}, f32[1,256]{1,0:T(1,128)S(1)}, u32[]{:S(2)}) copy-start(f32[1,256]{1,0:T(1,128)S(1)} %get-tuple-element.452) | copy-start | bytes 3076
  3.8 408.3 %copy-start.23 = (f32[1,256]{1,0:T(1,128)}, f32[1,256]{1,0:T(1,128)S(1)}, u32[]{:S(2)}) copy-start(f32[1,256]{1,0:T(1,128)S(1)} %get-tuple-element.453) | copy-start | bytes 3076
  11.6 73.4 %collective-permute-start = (f32[70,256]{1,0:T(8,128)S(1)}, f32[70,256]{1,0:T(8,128)S(1)}, u32[]{:S(2)}, u32[]{:S(2)}) collective-permute-start(f32[70,256]{1,0:T(8,128)S(1)} %pad_maximum_fusion.2), channel_id=1, source_target_pairs={{0,1},{1,0},{2,3},{3,2},{4,5},{5,4},{6,7},{7,6},{8,9},{9,8},{10,11... | collective-permute-start | bytes 215048 | tf_op jit(solution)/shard_map/ppermute | solution.py:10
  12.1 278.2 %copy-start.8 = (pred[256]{0:T(512)(128)(4,1)}, pred[256]{0:T(512)(128)(4,1)S(1)}, u32[]{:S(2)}) copy-start(pred[256]{0:T(512)(128)(4,1)S(1)} %compare_and_fusion.3) | copy-start | bytes 772
  12.1 288.7 %copy-start.6 = (pred[256]{0:T(512)(128)(4,1)}, pred[256]{0:T(512)(128)(4,1)S(1)}, u32[]{:S(2)}) copy-start(pred[256]{0:T(512)(128)(4,1)S(1)} %compare_and_fusion.2) | copy-start | bytes 772
  90.7 5.5 collective-permute-start.1
  101.9 4.4 collective-permute-start.2
  112.1 5.3 collective-permute-start.3
  217.1 72.1 %collective-permute-start.4 = (f32[70,256]{1,0:T(8,128)S(1)}, f32[70,256]{1,0:T(8,128)S(1)}, u32[]{:S(2)}, u32[]{:S(2)}) collective-permute-start(f32[70,256]{1,0:T(8,128)S(1)} %pad_maximum_fusion.1), channel_id=1, source_target_pairs={{0,1},{1,0},{2,3},{3,2},{4,5},{5,4},{6,7},{7,6},{8,9},{9,8},{10,11... | collective-permute-start | bytes 215048 | tf_op jit(solution)/shard_map/ppermute | solution.py:10
  295.0 4.7 collective-permute-start.5
  305.5 4.4 collective-permute-start.6
  315.7 5.3 collective-permute-start.7
  419.0 72.7 %collective-permute-start.8 = (f32[70,256]{1,0:T(8,128)S(1)}, f32[70,256]{1,0:T(8,128)S(1)}, u32[]{:S(2)}, u32[]{:S(2)}) collective-permute-start(f32[70,256]{1,0:T(8,128)S(1)} %pad_maximum_fusion), channel_id=1, source_target_pairs={{0,1},{1,0},{2,3},{3,2},{4,5},{5,4},{6,7},{7,6},{8,9},{9,8},{10,11... | collective-permute-start | bytes 215048 | tf_op jit(solution)/shard_map/ppermute | solution.py:10
  497.4 5.8 copy-start.7
  497.5 4.7 collective-permute-start.9
  508.1 4.4 collective-permute-start.10
  518.3 5.3 collective-permute-start.11
  534.3 4.9 copy-start.32
  534.3 4.9 copy-start.34
  534.3 4.9 copy-start.36
  534.4 4.9 copy-start.38
  534.4 4.9 copy-start.40
  543.6 4.9 copy-start.43
  543.7 4.9 copy-start.44
  543.7 4.9 copy-start.45
  543.7 4.9 copy-start.46
  543.7 4.9 copy-start.47
  543.7 4.9 copy-start.48
  553.0 5.0 copy-start.14
  553.0 5.0 copy-start.16
  553.0 5.0 copy-start.18
  553.0 5.0 copy-start.20
  553.0 5.0 copy-start.22
  553.0 5.0 copy-start.24
  553.0 5.0 copy-start.25
  553.0 5.0 copy-start.26
  553.0 5.0 copy-start.27
  553.0 5.0 copy-start.28
  553.1 5.0 copy-start.29
  553.1 5.0 copy-start.30
  562.4 37.8 %copy-start.51 = (f32[64]{0:T(128)S(1)}, f32[64]{0:T(128)}, u32[]{:S(2)}) copy-start(f32[64]{0:T(128)} %copy-done.50) | copy-start | bytes 772
  562.4 37.8 %copy-start.12 = (f32[64]{0:T(128)S(1)}, f32[64]{0:T(128)}, u32[]{:S(2)}) copy-start(f32[64]{0:T(128)} %copy-done.11) | copy-start | bytes 772
  (16 other events, 54.3 us)
